TPU v7x, 32 devices: a whole 2x2x4 slice. The times are simulated.
32 devices in a mesh: dp: 8 (over z, x), tensor: 4 (over y, core).
Axes of the slice: x: 2, y: 2, z: 4, core: 2. Of those that a mesh axis runs over, the one named last changes fastest.
Arguments:
- hidden_in: bfloat16 [32768, 768], P(('dp', 'tensor')), may hold values from -6 to 6
- cotangent: bfloat16 [32768, 768], P(('dp', 'tensor')), may hold values from -6 to 6
- lengths: int32 [32], P('dp'), may hold values from 31 to 1024, as said below
- latent: int32 [32, 1024], P('dp'), may hold values from 0 to 1, as said below
- ln1_gain: float32 [768], replicated, may hold values from 0.5 to 1.5
- ln1_bias: float32 [768], replicated, may hold values from -1.75 to 1.75
- w_qkv: float32 [3, 768, 768], P(None, 'dp', 'tensor'), may hold values from -0.3125 to 0.3125
- b_qv: float32 [2, 768], replicated, may hold values from -1.75 to 1.75
- w_out: float32 [768, 768], P('tensor', 'dp'), may hold values from -1.25 to 1.25
- b_out: float32 [768], replicated, may hold values from -1.75 to 1.75
- ln2_gain: float32 [768], replicated, may hold values from 0.5 to 1.5
- ln2_bias: float32 [768], replicated, may hold values from -1.75 to 1.75
- w_up: float32 [768, 3072], P('dp', 'tensor'), may hold values from -0.21875 to 0.21875
- b_up: float32 [3072], replicated, may hold values from -1.75 to 1.75
- w_down: float32 [3072, 768], P('tensor', 'dp'), may hold values from -0.109375 to 0.109375
- b_down: float32 [768], replicated, may hold values from -1.75 to 1.75
Outputs:
- hidden_out: bfloat16 [32768, 768], P(('dp', 'tensor'))
- grad_in: float32 [32768, 768], P(('dp', 'tensor'))
- grad_ln1_gain: float32 [768], replicated
- grad_ln1_bias: float32 [768], replicated
- grad_w_qkv: float32 [3, 768, 768], P(None, 'dp', 'tensor')
- grad_b_qv: float32 [2, 768], replicated
- grad_w_out: float32 [768, 768], P('tensor', 'dp')
- grad_b_out: float32 [768], replicated
- grad_ln2_gain: float32 [768], replicated
- grad_ln2_bias: float32 [768], replicated
- grad_w_up: float32 [768, 3072], P('dp', 'tensor')
- grad_b_up: float32 [3072], replicated
- grad_w_down: float32 [3072, 768], P('tensor', 'dp')
- grad_b_down: float32 [768], replicated
Inputs may be any that keep to these rules, and one draw needn't show every extreme that they name: `lengths`: A sequence's true length: a question of about 1024*30/1024 to 1024*400/1024 tokens, 0 to 6 latent thoughts and an answer, at most 1024; some sequence has exactly 1024, and some sequence has the shortest length, a shortest question and a one-token answer. `latent`: latent thoughts directly follow a sequence's question and lie within its true length.
All inputs are finite; a program needn't handle non-finite values.
Results may differ from a plain program's by a relative error of at most 0.015.
The roundings to bfloat16 on the way count: a program that leaves them out, or rounds other values in their place, can miss the bound.
Values may be sent and summed in bfloat16 or wider, within the bound.
No kernel may reach another device: no remote copies, remote signals or barrier semaphores. Data moves between devices by JAX's collectives and lax.ppermute only.
A program may use at most 320 MiB of HBM per device.

v0:
```python
import jax
import jax.numpy as jnp
from jax import lax
from jax.sharding import PartitionSpec as P

HEAD_DIM = 64
LEN = 1024


NEG_BIG = -1e30
EPSILON = 1e-05


def layer_norm(rows_in, gain, bias):
    center = rows_in - jnp.mean(rows_in, axis=-1, keepdims=True)
    spread = jnp.mean(center * center, axis=-1, keepdims=True)
    return center * lax.rsqrt(spread + EPSILON) * gain + bias


def gelu_tanh(values):
    return jax.nn.gelu(values, approximate=True)


def masked_scores(q_block, k_all, offset, length):
    score_scale = HEAD_DIM ** (-0.5)
    scores = (
        jnp.einsum("qhd,khd->hqk", q_block, k_all, preferred_element_type=jnp.float32) * score_scale
    )
    grid_shape = (q_block.shape[0], k_all.shape[0])
    q_pos = offset + lax.broadcasted_iota(jnp.int32, grid_shape, 0)
    k_pos = lax.broadcasted_iota(jnp.int32, grid_shape, 1)
    allowed = (k_pos <= q_pos) & (k_pos < length)
    return jnp.where(allowed[None], scores, NEG_BIG)


def attend_forward(packed):
    q_seq, k_seq, v_seq, length = packed
    head_count = q_seq.shape[1] // HEAD_DIM
    q_heads = q_seq.reshape(LEN, head_count, HEAD_DIM)
    k_heads = k_seq.reshape(LEN, head_count, HEAD_DIM)
    v_heads = v_seq.reshape(LEN, head_count, HEAD_DIM)
    block_rows = min(512, LEN)
    out_parts = []
    lse_parts = []
    for offset in range(0, LEN, block_rows):
        scores = masked_scores(q_heads[offset : offset + block_rows], k_heads, offset, length)
        row_peak = jnp.max(scores, axis=-1, keepdims=True)
        shifted = jnp.exp(scores - row_peak)
        totals = jnp.sum(shifted, axis=-1, keepdims=True)
        prob_low = (shifted / totals).astype(jnp.bfloat16)
        out_parts.append(
            jnp.einsum("hqk,khd->qhd", prob_low, v_heads, preferred_element_type=jnp.float32)
        )
        lse_parts.append((row_peak + jnp.log(totals))[:, :, 0])
    attended = jnp.concatenate(out_parts, axis=0).reshape(LEN, head_count * HEAD_DIM)
    return (attended, jnp.concatenate(lse_parts, axis=1))


def attend_backward(packed):
    q_seq, k_seq, v_seq, dout_seq, log_totals, length = packed
    head_count = q_seq.shape[1] // HEAD_DIM
    score_scale = HEAD_DIM ** (-0.5)
    q_heads = q_seq.reshape(LEN, head_count, HEAD_DIM)
    k_heads = k_seq.reshape(LEN, head_count, HEAD_DIM)
    v_heads = v_seq.reshape(LEN, head_count, HEAD_DIM)
    dout_heads = dout_seq.reshape(LEN, head_count, HEAD_DIM)
    block_rows = min(512, LEN)
    dk_acc = jnp.zeros((LEN, head_count, HEAD_DIM), jnp.float32)
    dv_acc = jnp.zeros((LEN, head_count, HEAD_DIM), jnp.float32)
    dq_parts = []
    for offset in range(0, LEN, block_rows):
        q_block = q_heads[offset : offset + block_rows]
        dout_block = dout_heads[offset : offset + block_rows]
        scores = masked_scores(q_block, k_heads, offset, length)
        probs = jnp.exp(scores - log_totals[:, offset : offset + block_rows, None])
        prob_low = probs.astype(jnp.bfloat16)
        d_prob = jnp.einsum("qhd,khd->hqk", dout_block, v_heads, preferred_element_type=jnp.float32)
        row_dot = jnp.sum(d_prob * probs, axis=-1, keepdims=True)
        d_score = (probs * (d_prob - row_dot)).astype(jnp.bfloat16)
        dq_parts.append(
            jnp.einsum("hqk,khd->qhd", d_score, k_heads, preferred_element_type=jnp.float32)
            * score_scale
        )
        dk_acc = (
            dk_acc
            + jnp.einsum("hqk,qhd->khd", d_score, q_block, preferred_element_type=jnp.float32)
            * score_scale
        )
        dv_acc = dv_acc + jnp.einsum(
            "hqk,qhd->khd", prob_low, dout_block, preferred_element_type=jnp.float32
        )
    col_count = head_count * HEAD_DIM
    return (
        jnp.concatenate(dq_parts, axis=0).reshape(LEN, col_count),
        dk_acc.reshape(LEN, col_count),
        dv_acc.reshape(LEN, col_count),
    )


def body(
    hidden_in,
    cotangent,
    lengths,
    latent,
    ln1_gain,
    ln1_bias,
    w_qkv,
    b_qv,
    w_out,
    b_out,
    ln2_gain,
    ln2_bias,
    w_up,
    b_up,
    w_down,
    b_down,
):
    t_index = lax.axis_index("tensor")
    own_rows = hidden_in.shape[0]
    own_seqs = own_rows // LEN
    qkv_weight, out_weight, up_weight, down_weight = (
        lax.all_gather(w_qkv.astype(jnp.bfloat16), "dp", axis=1, tiled=True),
        lax.all_gather(w_out.astype(jnp.bfloat16), "dp", axis=1, tiled=True),
        lax.all_gather(w_up.astype(jnp.bfloat16), "dp", axis=0, tiled=True),
        lax.all_gather(w_down.astype(jnp.bfloat16), "dp", axis=1, tiled=True),
    )
    own_lengths = lax.dynamic_slice_in_dim(lengths, t_index * own_seqs, own_seqs, 0)
    own_latent = lax.dynamic_slice_in_dim(latent, t_index * own_seqs, own_seqs, 0)
    qkv_weight, out_weight, up_weight, down_weight = (
        lax.all_gather(qkv_weight, "tensor", axis=2, tiled=True),
        lax.all_gather(out_weight, "tensor", axis=0, tiled=True),
        lax.all_gather(up_weight, "tensor", axis=1, tiled=True),
        lax.all_gather(down_weight, "tensor", axis=0, tiled=True),
    )
    positions = lax.broadcasted_iota(jnp.int32, (own_seqs, LEN), 1)
    keep_mask = (
        ((positions < own_lengths[:, None]) & (own_latent == 0))
        .astype(jnp.float32)
        .reshape(own_rows, 1)
    )
    x_rows = hidden_in.astype(jnp.float32)
    normed_low = layer_norm(x_rows, ln1_gain, ln1_bias).astype(jnp.bfloat16)
    group_rows = normed_low.shape[0]
    group_seqs = group_rows // LEN
    projected = jnp.einsum(
        "td,cde->cte", normed_low, qkv_weight, preferred_element_type=jnp.float32
    )
    q_low = (projected[0] + b_qv[0]).astype(jnp.bfloat16)
    k_low = projected[1].astype(jnp.bfloat16)
    v_low = (projected[2] + b_qv[1]).astype(jnp.bfloat16)

    def by_seq(row_array):
        return row_array.reshape(group_seqs, LEN, row_array.shape[1])

    attended, log_totals = lax.map(
        attend_forward, (by_seq(q_low), by_seq(k_low), by_seq(v_low), own_lengths)
    )
    attended_low = attended.reshape(group_rows, -1).astype(jnp.bfloat16)
    rows_part = attended_low
    attn_rows = jnp.dot(rows_part, out_weight, preferred_element_type=jnp.float32)
    resid_one = x_rows + attn_rows + b_out
    norm_two_low = layer_norm(resid_one, ln2_gain, ln2_bias).astype(jnp.bfloat16)
    pre_act = jnp.dot(norm_two_low, up_weight, preferred_element_type=jnp.float32) + b_up
    act_low = gelu_tanh(pre_act).astype(jnp.bfloat16)
    rows_part = act_low
    mlp_rows = jnp.dot(rows_part, down_weight, preferred_element_type=jnp.float32)
    hidden_out = (resid_one + mlp_rows + b_down).astype(jnp.bfloat16)
    d_out = cotangent.astype(jnp.float32) * keep_mask
    d_out_low = d_out.astype(jnp.bfloat16)
    g_down = jnp.einsum("tf,td->fd", act_low, d_out_low, preferred_element_type=jnp.float32)
    d_act = jnp.einsum("td,fd->tf", d_out_low, down_weight, preferred_element_type=jnp.float32)
    gelu_back = jax.vjp(gelu_tanh, pre_act)[1]
    d_pre_low = gelu_back(d_act)[0].astype(jnp.bfloat16)
    g_up = jnp.einsum("td,tf->df", norm_two_low, d_pre_low, preferred_element_type=jnp.float32)
    g_bias_up = jnp.sum(d_pre_low, axis=0, dtype=jnp.float32)
    rows_part = d_pre_low
    d_norm_two = jnp.einsum("tf,df->td", rows_part, up_weight, preferred_element_type=jnp.float32)
    ln_two_back = jax.vjp(layer_norm, resid_one, ln2_gain, ln2_bias)[1]
    d_resid_ln, g_ln2_gain, g_ln2_bias = ln_two_back(d_norm_two)
    d_resid = d_out + d_resid_ln
    g_b_down = jnp.sum(d_out, axis=0)
    g_b_out = jnp.sum(d_resid, axis=0)
    d_resid_low = d_resid.astype(jnp.bfloat16)
    g_out_w = jnp.einsum("tc,td->cd", attended_low, d_resid_low, preferred_element_type=jnp.float32)
    d_attended = jnp.einsum(
        "td,cd->tc", d_resid_low, out_weight, preferred_element_type=jnp.float32
    ).astype(jnp.bfloat16)
    d_q, d_k, d_v = lax.map(
        attend_backward,
        (by_seq(q_low), by_seq(k_low), by_seq(v_low), by_seq(d_attended), log_totals, own_lengths),
    )
    d_proj_low = jnp.stack(
        [d_q.reshape(group_rows, -1), d_k.reshape(group_rows, -1), d_v.reshape(group_rows, -1)]
    ).astype(jnp.bfloat16)
    g_qkv = jnp.einsum("td,cte->cde", normed_low, d_proj_low, preferred_element_type=jnp.float32)
    g_bias_qv = jnp.stack(
        [
            jnp.sum(d_proj_low[0], axis=0, dtype=jnp.float32),
            jnp.sum(d_proj_low[2], axis=0, dtype=jnp.float32),
        ]
    )
    rows_part = d_proj_low
    d_norm_one = jnp.einsum(
        "cte,cde->td", rows_part, qkv_weight, preferred_element_type=jnp.float32
    )
    ln_one_back = jax.vjp(layer_norm, x_rows, ln1_gain, ln1_bias)[1]
    d_x_ln, g_ln1_gain, g_ln1_bias = ln_one_back(d_norm_one)
    grad_in = d_resid + d_x_ln
    g_qkv, g_out_w, g_up, g_down = (
        lax.psum_scatter(
            g_qkv.astype(jnp.bfloat16), "tensor", scatter_dimension=2, tiled=True
        ).astype(jnp.float32),
        lax.psum_scatter(
            g_out_w.astype(jnp.bfloat16), "tensor", scatter_dimension=0, tiled=True
        ).astype(jnp.float32),
        lax.psum_scatter(
            g_up.astype(jnp.bfloat16), "tensor", scatter_dimension=1, tiled=True
        ).astype(jnp.float32),
        lax.psum_scatter(
            g_down.astype(jnp.bfloat16), "tensor", scatter_dimension=0, tiled=True
        ).astype(jnp.float32),
    )
    g_qkv, g_out_w, g_up, g_down = (
        lax.psum_scatter(g_qkv, "dp", scatter_dimension=1, tiled=True),
        lax.psum_scatter(g_out_w, "dp", scatter_dimension=1, tiled=True),
        lax.psum_scatter(g_up, "dp", scatter_dimension=0, tiled=True),
        lax.psum_scatter(g_down, "dp", scatter_dimension=1, tiled=True),
    )
    summed = lax.psum(
        (g_ln1_gain, g_ln1_bias, g_bias_qv, g_b_out, g_ln2_gain, g_ln2_bias, g_bias_up, g_b_down),
        ("dp", "tensor"),
    )
    return (
        hidden_out,
        grad_in,
        summed[0],
        summed[1],
        g_qkv,
        summed[2],
        g_out_w,
        summed[3],
        summed[4],
        summed[5],
        g_up,
        summed[6],
        g_down,
        summed[7],
    )


def solution(mesh):
    placed = (
        P(("dp", "tensor"), None),
        P(("dp", "tensor"), None),
        P("dp"),
        P("dp", None),
        P(),
        P(),
        P(None, "dp", "tensor"),
        P(),
        P("tensor", "dp"),
        P(),
        P(),
        P(),
        P("dp", "tensor"),
        P(),
        P("tensor", "dp"),
        P(),
    )
    return jax.shard_map(
        body,
        mesh=mesh,
        in_specs=placed,
        out_specs=(
            P(("dp", "tensor"), None),
            P(("dp", "tensor"), None),
            P(),
            P(),
            P(None, "dp", "tensor"),
            P(),
            P("tensor", "dp"),
            P(),
            P(),
            P(),
            P("dp", "tensor"),
            P(),
            P("tensor", "dp"),
            P(),
        ),
        check_vma=False,
    )
```

profile of v0, /device:TPU:0, one launch (start us, length us, event | category | flops | bytes accessed | tf_op | source)
XLA Modules:
  0.0 868.7 jit_solution(17949149070958209953)
XLA Ops:
  11.8 43.5 %all_gather.24 = bf16[3,768,192]{2,0,1:T(4,128)(2,1)S(1)} all-gather(bf16[3,96,192]{2,0,1:T(4,128)(2,1)S(1)} %copy.90), channel_id=1, replica_groups=mesh['dp'=8,'tensor'=4] {'dp'}, dimensions={1}, use_global_device_ids=true | all-gather | bytes 995328 | tf_op jit(solution)/shard_map/all_gather | solution.py:122
  57.5 31.4 %all_gather.26 = bf16[192,768]{0,1:T(8,128)(2,1)S(1)} all-gather(bf16[192,96]{0,1:T(8,128)(2,1)S(1)} %copy.93), channel_id=1, replica_groups=mesh['dp'=8,'tensor'=4] {'dp'}, dimensions={1}, use_global_device_ids=true | all-gather | bytes 331776 | tf_op jit(solution)/shard_map/all_gather | solution.py:123
  106.4 31.6 %all-gather.7.cloned.1.call-done = bf16[3,768,768]{1,2,0:T(8,128)(2,1)} async-done(((bf16[3,768,192]{1,2,0:T(8,128)(2,1)}), bf16[3,768,768]{1,2,0:T(8,128)(2,1)}) %all-gather.7.cloned.1.call-update) | async-done | bytes 3538960 | tf_op jit(solution)/shard_map/all_gather | solution.py:130
  151.0 10.9 %fusion.19 = (f32[12,512]{1,0:T(8,128)S(1)}, f32[12,512,1024]{2,1,0:T(8,128)}) fusion(pred[512,1024]{1,0:T(8,128)(4,1)S(1)} %get-tuple-element.142, bf16[512,12,64]{0,2,1:T(8,128)(2,1)S(1)} %bitcast.93, bf16[1024,12,64]{0,2,1:T(8,128)(2,1)S(1)} %bitcast.82), kind=kOutput, calls=%fused_computation.33 | convolution fusion | flops 824174592 | bytes 28073984 | tf_op jit(solution)/shard_map/while/body/eval_jaxpr/qhd,khd->hqk/dot_general | solution.py:27
  161.9 13.4 %fusion = f32[12,512]{1,0:T(8,128)S(1)} fusion(f32[12,512]{1,0:T(8,128)S(1)} %get-tuple-element.146, f32[12,512,1024]{2,1,0:T(8,128)} %get-tuple-element.147, pred[512,1024]{1,0:T(8,128)(4,1)S(1)} %get-tuple-element.142), kind=kLoop, calls=%fused_computation.12 | loop fusion | flops 25159680 | bytes 25739264 | tf_op jit(solution)/shard_map/while/body/eval_jaxpr/reduce_sum | solution.py:49
  187.5 10.8 %fusion.20 = (f32[12,512]{1,0:T(8,128)S(1)}, f32[12,512,1024]{2,1,0:T(8,128)}) fusion(pred[512,1024]{1,0:T(8,128)(4,1)S(1)} %get-tuple-element.143, bf16[512,12,64]{0,2,1:T(8,128)(2,1)S(1)} %bitcast.90, bf16[1024,12,64]{0,2,1:T(8,128)(2,1)S(1)} %bitcast.83), kind=kOutput, calls=%fused_computation.34 | convolution fusion | flops 824174592 | bytes 28073984 | tf_op jit(solution)/shard_map/while/body/eval_jaxpr/qhd,khd->hqk/dot_general | solution.py:27
  198.3 13.2 %fusion.1 = f32[12,512]{1,0:T(8,128)S(1)} fusion(f32[12,512]{1,0:T(8,128)S(1)} %get-tuple-element.144, f32[12,512,1024]{2,1,0:T(8,128)} %get-tuple-element.145, pred[512,1024]{1,0:T(8,128)(4,1)S(1)} %get-tuple-element.143), kind=kLoop, calls=%fused_computation.13 | loop fusion | flops 25159680 | bytes 25739264 | tf_op jit(solution)/shard_map/while/body/eval_jaxpr/reduce_sum | solution.py:49
  229.5 10.5 %fusion.70 = f32[1024,3072]{1,0:T(8,128)} fusion(bf16[768,3072]{1,0:T(8,128)(2,1)} %all-gather.13.cloned.1.call-done, f32[1024,768]{0,1:T(8,128)S(1)} %get-tuple-element.149, f32[768]{0:T(1024)S(1)} %copy-done.31, f32[768]{0:T(1024)S(1)} %copy-done.30, f32[1024]{0:T(1024)S(1)} %fusion.58, f32[1024]{0:T(1024)S(1)} %broadcast_multiply_fusion), kind=kOutput, calls=%fused_computation.127 | convolution fusion | flops 4835770368 | bytes 20461568 | tf_op jit(solution)/shard_map/dot_general | solution.py:163
  240.0 18.4 %convert_reduce_fusion = (f32[3072]{0:T(1024)}, bf16[1024,3072]{1,0:T(8,128)(2,1)S(1)}) fusion(f32[1024,3072]{1,0:T(8,128)} %fusion.70, f32[3072]{0:T(1024)S(1)} %copy-done.49, bf16[3072,768]{0,1:T(8,128)(2,1)} %all-gather.17.cloned.1.call-done, bf16[1024,768]{0,1:T(8,128)(2,1)} %copy.96, f32[1024]{0:T(1024)S(1)} %bitcast.105), kind=kOutput, calls=%fused_computation.27 | convolution fusion | flops 4906546176 | bytes 25194496 | tf_op jit(solution)/shard_map/td,fd->tf/dot_general | solution.py:171
  285.9 13.3 %fusion.11 = f32[12,64,1024]{2,1,0:T(8,128)} fusion(bf16[512,12,64]{0,2,1:T(8,128)(2,1)S(1)} %bitcast.99, f32[12,512]{1,0:T(8,128)S(1)} %log_add_fusion, f32[12,512,1024]{2,1,0:T(8,128)} %get-tuple-element.145, pred[512,1024]{1,0:T(8,128)(4,1)S(1)} %copy-done.13), kind=kOutput, calls=%fused_computation.25 | convolution fusion | flops 830472192 | bytes 29646848 | tf_op jit(solution)/shard_map/while/body/eval_jaxpr/hqk,qhd->khd/dot_general | solution.py:89
  299.1 18.2 %multiply_reduce_fusion = (f32[12,512]{1,0:T(8,128)S(1)}, f32[12,512,1024]{2,1,0:T(8,128)}) fusion(f32[12,512]{1,0:T(8,128)S(1)} %log_add_fusion, f32[12,512,1024]{2,1,0:T(8,128)} %get-tuple-element.145, pred[512,1024]{1,0:T(8,128)(4,1)} %copy-done.12, bf16[512,12,64]{0,2,1:T(8,128)(2,1)} %bitcast.100, bf16[1024,12,64]{0,2,1:T(8,128)(2,1)} %copy-done.9), kind=kOutput, calls=%fused_computation.1 | convolution fusion | flops 836757504 | bytes 53264384 | tf_op jit(solution)/shard_map/while/body/eval_jaxpr/qhd,khd->hqk/dot_general | solution.py:77
  317.4 18.7 %multiply_reduce_fusion.1 = (f32[12,512]{1,0:T(8,128)S(1)}, f32[12,512,1024]{2,1,0:T(8,128)}) fusion(f32[12,512]{1,0:T(8,128)S(1)} %log_add_fusion.1, f32[12,512,1024]{2,1,0:T(8,128)} %get-tuple-element.147, pred[512,1024]{1,0:T(8,128)(4,1)} %copy-done.11, bf16[512,12,64]{0,2,1:T(8,128)(2,1)} %bitcast.97, bf16[1024,12,64]{0,2,1:T(8,128)(2,1)} %copy-done.9), kind=kOutput, calls=%fused_computation.4 | convolution fusion | flops 836757504 | bytes 53264384 | tf_op jit(solution)/shard_map/while/body/eval_jaxpr/qhd,khd->hqk/dot_general | solution.py:77
  336.1 14.2 %add_convert_fusion = bf16[12,64,1024]{2,1,0:T(8,128)(2,1)} fusion(f32[12,64,1024]{2,1,0:T(8,128)} %fusion.11, bf16[512,12,64]{0,2,1:T(8,128)(2,1)} %bitcast.98, f32[12,512]{1,0:T(8,128)S(1)} %log_add_fusion.1, f32[12,512,1024]{2,1,0:T(8,128)} %get-tuple-element.147, pred[512,1024]{1,0:T(8,128)(4,1)} %copy-done.11), kind=kOutput, calls=%fused_computation.65 | convolution fusion | flops 832045056 | bytes 31219712 | tf_op jit(solution)/shard_map/while/body/eval_jaxpr/hqk,qhd->khd/dot_general | solution.py:89
  352.9 42.7 %multiply_convert_fusion = (bf16[12,512,1024]{2,1,0:T(8,128)(2,1)}, bf16[12,512,1024]{2,1,0:T(8,128)(2,1)}) fusion(f32[12,512,1024]{2,1,0:T(8,128)} %get-tuple-element.153, f32[12,512]{1,0:T(8,128)S(1)} %get-tuple-element.152, f32[12,512]{1,0:T(8,128)S(1)} %log_add_fusion, f32[12,512,1024]{2,1,0:T(8,128)} %get-tuple-element.145, ...), kind=kLoop, calls=%fused_computation | loop fusion | flops 75497472 | bytes 126976000 | tf_op jit(solution)/shard_map/while/body/eval_jaxpr/convert_element_type | solution.py:79
  440.9 13.7 %convolution_convert_fusion = bf16[3072,768]{1,0:T(8,128)(2,1)} fusion(bf16[1024,768]{0,1:T(8,128)(2,1)} %copy.96, f32[1024]{0:T(1024)S(1)} %bitcast.107, f32[1024,3072]{1,0:T(8,128)} %fusion.70, f32[3072]{0:T(1024)S(1)} %copy-done.49), kind=kOutput, calls=%fused_computation.35 | convolution fusion | flops 4868014080 | bytes 18890752 | tf_op jit(solution)/shard_map/tf,td->fd/dot_general | solution.py:170
  455.3 9.7 %convolution_convert_fusion.1 = bf16[768,3072]{1,0:T(8,128)(2,1)} fusion(bf16[1024,3072]{1,0:T(8,128)(2,1)} %copy-done.55, f32[1024,768]{0,1:T(8,128)S(1)} %get-tuple-element.149, f32[768]{0:T(1024)S(1)} %copy-done.32, f32[768]{0:T(1024)S(1)} %copy-done.30, f32[1024]{0:T(1024)S(1)} %fusion.58, f32[1024]{0:T(1024)S(1)} %broadcast_multiply_fusion), kind=kOutput, calls=%fused_computation.36 | convolution fusion | flops 4838129664 | bytes 14170112 | tf_op jit(solution)/shard_map/td,tf->df/dot_general | solution.py:174
  467.2 14.2 %reduce-scatter.15.cloned.1.call-done = bf16[3,768,192]{1,2,0:T(8,128)(2,1)} async-done(((bf16[3,768,768]{1,2,0:T(8,128)(2,1)}), bf16[3,768,192]{1,2,0:T(8,128)(2,1)}) %reduce-scatter.15.cloned.1.call-update) | async-done | bytes 884752 | tf_op jit(solution)/shard_map/reduce_scatter | solution.py:210
  489.7 42.1 %reduce-scatter.23.cloned.1.call-done = bf16[768,768]{1,0:T(8,128)(2,1)} async-done(((bf16[3072,768]{1,0:T(8,128)(2,1)}), bf16[768,768]{1,0:T(8,128)(2,1)}) %reduce-scatter.23.cloned.1.call-update) | async-done | bytes 1179664 | tf_op jit(solution)/shard_map/reduce_scatter | solution.py:219
  534.6 47.6 %reduce-scatter.19.cloned.1.call-done = bf16[768,768]{1,0:T(8,128)(2,1)} async-done(((bf16[768,3072]{1,0:T(8,128)(2,1)}), bf16[768,768]{1,0:T(8,128)(2,1)}) %reduce-scatter.19.cloned.1.call-update) | async-done | bytes 1179664 | tf_op jit(solution)/shard_map/reduce_scatter | solution.py:216
  585.1 10.9 %add_convert_fusion.1 = bf16[1024,768]{0,1:T(8,128)(2,1)} fusion(f32[1024,768]{0,1:T(8,128)S(1)} %get-tuple-element.149, bf16[3072,768]{0,1:T(8,128)(2,1)} %all-gather.17.cloned.1.call-done, f32[768]{0:T(1024)S(1)} %copy-done.53, f32[1024,3072]{1,0:T(8,128)} %fusion.70, f32[3072]{0:T(1024)S(1)} %copy-done.49), kind=kOutput, calls=%fused_computation.72 | convolution fusion | flops 4865654784 | bytes 22035456 | tf_op jit(solution)/shard_map/dot_general | solution.py:166
  623.3 41.0 %all-reduce = (f32[768]{0:T(1024)}, f32[768]{0:T(1024)}, f32[2,768]{1,0:T(2,128)}, f32[768]{0:T(1024)}, f32[768]{0:T(1024)}, /*index=5*/f32[768]{0:T(1024)}, f32[3072]{0:T(1024)}, f32[768]{0:T(1024)}) all-reduce(f32[768]{0:T(1024)S(1)} %get-tuple-element.123, ...), channel_id=1, replica_groups=mesh['dp'=8,'tensor'=4] {'dp','tensor'}, use_global_device_ids=true, to_apply=%region_15.16 | all-reduce | flops 9216 | bytes 73728 | tf_op jit(solution)/shard_map/psum | solution.py:229
  665.9 51.8 %reduce-scatter.25.cloned.1.call-done = f32[96,576]{1,0:T(8,128)} async-done(((f32[768,576]{1,0:T(8,128)}), f32[96,576]{1,0:T(8,128)}) %reduce-scatter.25.cloned.1.call-update) | async-done | bytes 221200
  719.5 70.1 %reduce-scatter.29.cloned.1.call-done = f32[96,768]{1,0:T(8,128)} async-done(((f32[768,768]{1,0:T(8,128)}), f32[96,768]{1,0:T(8,128)}) %reduce-scatter.29.cloned.1.call-update) | async-done | bytes 294928
  789.6 72.1 %reduce-scatter.21.cloned.1.call-done = f32[96,768]{1,0:T(8,128)} async-done(((f32[768,768]{1,0:T(8,128)}), f32[96,768]{1,0:T(8,128)}) %reduce-scatter.21.cloned.1.call-update) | async-done | bytes 294928 | tf_op jit(solution)/shard_map/reduce_scatter | solution.py:226
  (224 shorter events, 189.5 us)
Async XLA Ops:
  7.2 82.7 %all-gather.11.cloned.1.call-start = ((), (), s32[]{:S(2)}) async-start(), calls=%async_computation.10 | async-start | bytes 1327104 | tf_op jit(solution)/shard_map/all_gather | solution.py:124
  8.9 48.5 %copy-start.35 = (f32[192,96]{1,0:T(8,128)S(1)}, f32[192,96]{1,0:T(8,128)}, u32[]{:S(2)}) copy-start(f32[192,96]{1,0:T(8,128)} %param.24) | copy-start | bytes 221188
  8.9 97.5 %all-gather.15.cloned.1.call-start = ((), (), s32[]{:S(2)}) async-start(), calls=%async_computation.12 | async-start | bytes 1327104 | tf_op jit(solution)/shard_map/all_gather | solution.py:125
  10.6 127.5 %all-gather.7.cloned.1.call-start = ((), (), s32[]{:S(2)}) async-start(), calls=%async_computation.8 | async-start | bytes 4423680 | tf_op jit(solution)/shard_map/all_gather | solution.py:130
  57.3 167.6 %all-gather.9.cloned.1.call-start = ((), (), s32[]{:S(2)}) async-start(), calls=%async_computation.9 | async-start | bytes 1474560 | tf_op jit(solution)/shard_map/all_gather | solution.py:131
  89.8 139.5 %all-gather.13.cloned.1.call-start = ((), (), s32[]{:S(2)}) async-start(), calls=%async_computation.11 | async-start | bytes 5898240 | tf_op jit(solution)/shard_map/all_gather | solution.py:132
  90.4 149.6 %all-gather.17.cloned.1.call-start = ((), (), s32[]{:S(2)}) async-start(), calls=%async_computation.13 | async-start | bytes 5898240 | tf_op jit(solution)/shard_map/all_gather | solution.py:133
  91.3 46.8 %copy-start.3 = (bf16[1024,768]{0,1:T(8,128)(2,1)}, bf16[1024,768]{0,1:T(8,128)(2,1)S(1)}, u32[]{:S(2)}) copy-start(bf16[1024,768]{0,1:T(8,128)(2,1)S(1)} %copy.89) | copy-start | bytes 4718596
  94.5 43.6 %copy-start.38 = (f32[768]{0:T(1024)S(1)}, f32[768]{0:T(1024)}, u32[]{:S(2)}) copy-start(f32[768]{0:T(1024)} %param.20) | copy-start | bytes 9220
  94.5 43.6 %copy-start.51 = (f32[768]{0:T(1024)S(1)}, f32[768]{0:T(1024)}, u32[]{:S(2)}) copy-start(f32[768]{0:T(1024)} %param.21) | copy-start | bytes 9220
  98.0 46.3 %copy-start.33 = (f32[1024]{0:T(1024)}, f32[1024]{0:T(1024)S(1)}, u32[]{:S(2)}) copy-start(f32[1024]{0:T(1024)S(1)} %broadcast_multiply_fusion.1) | copy-start | bytes 12292
  99.0 45.3 %copy-start.36 = (f32[1024]{0:T(1024)}, f32[1024]{0:T(1024)S(1)}, u32[]{:S(2)}) copy-start(f32[1024]{0:T(1024)S(1)} %fusion.57) | copy-start | bytes 12292
  99.6 75.8 %copy-start.11 = (pred[512,1024]{1,0:T(8,128)(4,1)}, pred[512,1024]{1,0:T(8,128)(4,1)S(1)}, u32[]{:S(2)}) copy-start(pred[512,1024]{1,0:T(8,128)(4,1)S(1)} %get-tuple-element.142) | copy-start | bytes 1572868
  99.6 111.9 %copy-start.12 = (pred[512,1024]{1,0:T(8,128)(4,1)}, pred[512,1024]{1,0:T(8,128)(4,1)S(1)}, u32[]{:S(2)}) copy-start(pred[512,1024]{1,0:T(8,128)(4,1)S(1)} %get-tuple-element.143) | copy-start | bytes 1572868
  106.4 358.7 %reduce-scatter.17.cloned.1.call-start = ((), (), s32[]{:S(2)}) async-start(), calls=%async_computation.15 | async-start | bytes 1474560 | tf_op jit(solution)/shard_map/reduce_scatter | solution.py:213
  151.0 60.5 %copy-start.9 = (bf16[1024,12,64]{0,2,1:T(8,128)(2,1)}, bf16[1024,12,64]{0,2,1:T(8,128)(2,1)S(1)}, u32[]{:S(2)}) copy-start(bf16[1024,12,64]{0,2,1:T(8,128)(2,1)S(1)} %add_convert_fusion.3) | copy-start | bytes 4718596
  317.3 164.1 %reduce-scatter.15.cloned.1.call-start = ((), (), s32[]{:S(2)}) async-start(), calls=%async_computation.14 | async-start | bytes 4423680 | tf_op jit(solution)/shard_map/reduce_scatter | solution.py:210
  440.9 90.9 %reduce-scatter.23.cloned.1.call-start = ((), (), s32[]{:S(2)}) async-start(), calls=%async_computation.18 | async-start | bytes 5898240 | tf_op jit(solution)/shard_map/reduce_scatter | solution.py:219
  454.6 127.6 %reduce-scatter.19.cloned.1.call-start = ((), (), s32[]{:S(2)}) async-start(), calls=%async_computation.16 | async-start | bytes 5898240 | tf_op jit(solution)/shard_map/reduce_scatter | solution.py:216
  465.0 199.3 %reduce-scatter.27.cloned.1.call-start = ((), (), s32[]{:S(2)}) async-start(), calls=%async_computation.20 | async-start | bytes 884736
  467.2 250.5 %reduce-scatter.25.cloned.1.call-start = ((), (), s32[]{:S(2)}) async-start(), calls=%async_computation.19 | async-start | bytes 2211840
  489.7 300.0 %reduce-scatter.29.cloned.1.call-start = ((), (), s32[]{:S(2)}) async-start(), calls=%async_computation.21 | async-start | bytes 2654208
  534.5 50.6 %copy-start.53 = (f32[768]{0:T(1024)S(1)}, f32[768]{0:T(1024)}, u32[]{:S(2)}) copy-start(f32[768]{0:T(1024)} %param.31) | copy-start | bytes 9220
  534.5 327.2 %reduce-scatter.21.cloned.1.call-start = ((), (), s32[]{:S(2)}) async-start(), calls=%async_computation.17 | async-start | bytes 2654208 | tf_op jit(solution)/shard_map/reduce_scatter | solution.py:226
  (47 other events, 406.2 us)
Sparse Core Ops, SparseCore 0:
  10.8 51.9 all-gather.10
  65.5 40.8 all-gather.14
  108.5 29.5 all-gather.6
  140.1 17.4 all-gather.8
  159.0 37.4 all-gather.12
  197.9 37.4 all-gather.16
  317.5 25.7 reduce-scatter.16
  441.0 40.3 reduce-scatter.14
  484.0 47.8 reduce-scatter.22
  534.4 47.8 reduce-scatter.18
  585.5 62.4 reduce-scatter.26
  651.8 65.8 reduce-scatter.24
  721.7 67.8 reduce-scatter.28
  793.6 68.1 reduce-scatter.20
where the time goes:
time: 876 us; the launch traced here: 869 us
  waiting for transfers between devices  337 us (38%)
  matrix products  235 us (27%)
  blocking collectives  116 us (13%)
  other arithmetic  97.7 us (11%)
  local copies, waits for them, and re-layouts  67.7 us (8%)
  between operations  15.1 us (2%)
    unnamed x17, waiting for transfers between devices  123 us
    reduce_scatter x1, waiting for transfers between devices, body(): lax.psum_scatter(g_up, 'dp', scatter_dimension=0, tiled=True)  72.1 us
    reduce_scatter x1, waiting for transfers between devices, body(): lax.psum_scatter(g_up.astype(jnp.bfloat16), 'tensor', scatter_dimension=1...  47.6 us
    unnamed x124, local copies, waits for them, and re-layouts  45.1 us
    all_gather x1, blocking collectives, body(): lax.all_gather(w_qkv.astype(jnp.bfloat16), 'dp', axis=1, tiled=True)  43.5 us
    convert_element_type x1, other arithmetic, attend_backward(): d_score = (probs * (d_prob - row_dot)).astype(jnp.bfloat16)  42.7 us
    reduce_scatter x1, waiting for transfers between devices, body(): lax.psum_scatter(g_down.astype(jnp.bfloat16), 'tensor', scatter_dimension...  42.1 us
    psum x1, blocking collectives, body(): lax.psum((g_ln1_gain, g_ln1_bias, g_bias_qv, g_b_out, g_ln2_gain, g_ln2_b...  41 us
  transfers between devices with their start and end apart: 14, of which 8 were waited for; matrix products, arithmetic and copies ran while one was open for 35% of the time, Pallas kernels for 0%

commit v1 on v0

v1 whole, which is shorter than its diff:
```python
import functools

import jax
import jax.numpy as jnp
from jax import lax
from jax.experimental import pallas as pl
from jax.experimental.pallas import tpu as pltpu
from jax.sharding import PartitionSpec as P

HEAD_DIM = 64
LEN = 1024
PAIR = 2 * HEAD_DIM
TILE = 256
NEG_BIG = -1e30
EPSILON = 1e-05
VMEM_BYTES = 66_900_000
BF = jnp.bfloat16
F32 = jnp.float32
BOTH = ("dp", "tensor")


def dot_nn(a, b):
    return lax.dot_general(a, b, (((1,), (0,)), ((), ())), preferred_element_type=F32)


def dot_nt(a, b):
    return lax.dot_general(a, b, (((1,), (1,)), ((), ())), preferred_element_type=F32)


def dot_tn(a, b):
    return lax.dot_general(a, b, (((0,), (0,)), ((), ())), preferred_element_type=F32)


def norm_parts(rows_in):
    center = rows_in - jnp.mean(rows_in, axis=-1, keepdims=True)
    spread = jnp.mean(center * center, axis=-1, keepdims=True)
    scale = lax.rsqrt(spread + EPSILON)
    return center * scale, scale


def norm_back(gy, normed, scale):
    mean_gy = jnp.mean(gy, axis=-1, keepdims=True)
    mean_gyn = jnp.mean(gy * normed, axis=-1, keepdims=True)
    return (gy - mean_gy - normed * mean_gyn) * scale


def col_sum(values):
    return jnp.sum(values, axis=0, keepdims=True)


def once(shape, index):
    return pl.BlockSpec(shape, index, pipeline_mode=pl.Buffered(1))


def params():
    return pltpu.CompilerParams(
        dimension_semantics=("arbitrary",), vmem_limit_bytes=VMEM_BYTES
    )


def qkv_kernel(blocks, x_ref, gain_ref, bias_ref, bqv_ref, raw_ref, q_ref, k_ref, v_ref, n_ref, w_ref):
    width = x_ref.shape[1]

    @pl.when(pl.program_id(0) == 0)
    def _():
        def piece(t, c):
            return raw_ref[:, t, :, c * PAIR : (c + 1) * PAIR].reshape(width, PAIR)

        for t in range(blocks):
            for c in range(4):
                w_ref[c, :, t * PAIR : (t + 1) * PAIR] = piece(t, c)
        for u in range(blocks // 2):
            col = (blocks + u) * PAIR
            for half in range(2):
                left = piece(2 * u, 4 + half)
                right = piece(2 * u + 1, 4 + half)
                w_ref[2 * half, :, col : col + PAIR] = jnp.concatenate(
                    [left[:, :HEAD_DIM], right[:, :HEAD_DIM]], axis=1
                )
                w_ref[2 * half + 1, :, col : col + PAIR] = jnp.concatenate(
                    [left[:, HEAD_DIM:], right[:, HEAD_DIM:]], axis=1
                )

    normed, _ = norm_parts(x_ref[...].astype(F32))
    low = (normed * gain_ref[...] + bias_ref[...]).astype(BF)
    n_ref[...] = low
    q_low = (dot_nn(low, w_ref[0]) + bqv_ref[0:1, :]).astype(BF)
    q_ref[...] = q_low * BF(HEAD_DIM ** (-0.5))
    k_ref[...] = dot_nn(low, w_ref[1]).astype(BF)
    v_ref[...] = (dot_nn(low, w_ref[2]) + bqv_ref[1:2, :]).astype(BF)


def project(x, gain, bias, bqv, raw):
    rows, width = x.shape
    blocks = raw.shape[1]
    row_spec = pl.BlockSpec((TILE, width), lambda i: (i, 0))
    return pl.pallas_call(
        functools.partial(qkv_kernel, blocks),
        grid=(rows // TILE,),
        in_specs=[
            row_spec,
            once((1, width), lambda i: (0, 0)),
            once((1, width), lambda i: (0, 0)),
            once((2, width), lambda i: (0, 0)),
            once(raw.shape, lambda i: (0, 0, 0, 0)),
        ],
        out_specs=[row_spec] * 4 + [once((4, width, width), lambda i: (0, 0, 0))],
        out_shape=[jax.ShapeDtypeStruct((rows, width), BF)] * 4
        + [jax.ShapeDtypeStruct((4, width, width), BF)],
        compiler_params=params(),
        name="project",
    )(x, gain, bias, bqv, raw)


def half_masks():
    lane = lax.broadcasted_iota(jnp.int32, (1, PAIR), 1)
    first = (lane < HEAD_DIM).astype(F32)
    return first.astype(BF), (1.0 - first).astype(BF)


def attend_kernel(len_ref, q_ref, k_ref, v_ref, o_ref, lse_ref):
    rows = q_ref.shape[0]
    length = len_ref[0]
    masks = half_masks()
    lane = lax.broadcasted_iota(jnp.int32, (TILE, PAIR), 1)
    k_pos = lax.broadcasted_iota(jnp.int32, (1, rows), 1)
    bias = jnp.where(k_pos < length, 0.0, NEG_BIG)
    tri = lax.broadcasted_iota(jnp.int32, (TILE, TILE), 0) >= lax.broadcasted_iota(
        jnp.int32, (TILE, TILE), 1
    )
    for n in range(0, rows, TILE):
        q_block = q_ref[n : n + TILE, :]
        outs = []
        lses = []
        for mask in masks:
            q_one = q_block * mask
            s_diag = dot_nt(q_one, k_ref[n : n + TILE, :]) + bias[:, n : n + TILE]
            s_diag = jnp.where(tri, s_diag, NEG_BIG)
            peak = jnp.max(s_diag, axis=1, keepdims=True)
            if n:
                s_rest = dot_nt(q_one, k_ref[:n, :]) + bias[:, :n]
                peak = jnp.maximum(peak, jnp.max(s_rest, axis=1, keepdims=True))
            e_diag = jnp.exp(s_diag - peak)
            total = jnp.sum(e_diag, axis=1, keepdims=True)
            acc = dot_nn(e_diag.astype(BF), v_ref[n : n + TILE, :])
            if n:
                e_rest = jnp.exp(s_rest - peak)
                total = total + jnp.sum(e_rest, axis=1, keepdims=True)
                acc = acc + dot_nn(e_rest.astype(BF), v_ref[:n, :])
            outs.append(acc / total)
            lses.append(peak + jnp.log(total))
        o_ref[n : n + TILE, :] = jnp.where(lane < HEAD_DIM, outs[0], outs[1]).astype(BF)
        both = jnp.where(lane == 0, lses[0], jnp.where(lane == 1, lses[1], 0.0))
        lse_ref[0, :, n : n + TILE] = jnp.transpose(both)[:8, :]


def attend(lengths, q, k, v):
    rows, width = q.shape
    pairs = width // PAIR
    pair_spec = pl.BlockSpec((rows, PAIR), lambda i, *_: (0, i))
    return pl.pallas_call(
        attend_kernel,
        grid_spec=pltpu.PrefetchScalarGridSpec(
            num_scalar_prefetch=1,
            grid=(pairs,),
            in_specs=[pair_spec] * 3,
            out_specs=[pair_spec, pl.BlockSpec((1, 8, rows), lambda i, *_: (i, 0, 0))],
        ),
        out_shape=[
            jax.ShapeDtypeStruct((rows, width), BF),
            jax.ShapeDtypeStruct((pairs, 8, rows), F32),
        ],
        compiler_params=params(),
        name="attend",
    )(lengths, q, k, v)


def attend_back_kernel(
    len_ref, q_ref, k_ref, v_ref, o_ref, do_ref, lse_ref, dq_ref, dk_ref, dv_ref, dq_acc
):
    rows = q_ref.shape[0]
    length = len_ref[0]
    masks = half_masks()
    prod = jnp.transpose(do_ref[...].astype(F32) * o_ref[...].astype(F32))
    tri = lax.broadcasted_iota(jnp.int32, (TILE, TILE), 0) <= lax.broadcasted_iota(
        jnp.int32, (TILE, TILE), 1
    )
    k_pos = lax.broadcasted_iota(jnp.int32, (TILE, 1), 0)
    dq_acc[...] = jnp.zeros_like(dq_acc)
    heads = []
    for h, mask in enumerate(masks):
        heads.append(
            (
                mask,
                q_ref[...] * mask,
                do_ref[...] * mask,
                lse_ref[0, h : h + 1, :],
                jnp.sum(prod[h * HEAD_DIM : (h + 1) * HEAD_DIM, :], axis=0, keepdims=True),
            )
        )
    for n in range(0, rows, TILE):
        k_block = k_ref[n : n + TILE, :]
        v_block = v_ref[n : n + TILE, :]
        bias = jnp.where(k_pos + n < length, 0.0, NEG_BIG)
        dk = jnp.zeros((TILE, PAIR), F32)
        dv = jnp.zeros((TILE, PAIR), F32)
        for mask, q_one, do_one, lse, delta in heads:
            k_one = k_block * mask
            for low, high in ((n, n + TILE), (n + TILE, rows)):
                if low == high:
                    continue
                s = dot_nt(k_block, q_one[low:high]) + bias
                if low == n:
                    s = jnp.where(tri, s, NEG_BIG)
                p = jnp.exp(s - lse[:, low:high])
                dp = dot_nt(v_block, do_one[low:high])
                ds = (p * (dp - delta[:, low:high])).astype(BF)
                dv = dv + dot_nn(p.astype(BF), do_one[low:high])
                dk = dk + dot_nn(ds, q_one[low:high])
                dq_acc[low:high, :] += dot_tn(ds, k_one)
        dk_ref[n : n + TILE, :] = dk.astype(BF)
        dv_ref[n : n + TILE, :] = dv.astype(BF)
    dq_ref[...] = (dq_acc[...] * (HEAD_DIM ** (-0.5))).astype(BF)


def attend_back(lengths, q, k, v, out, d_out, lse):
    rows, width = q.shape
    pairs = width // PAIR
    pair_spec = pl.BlockSpec((rows, PAIR), lambda i, *_: (0, i))
    return pl.pallas_call(
        attend_back_kernel,
        grid_spec=pltpu.PrefetchScalarGridSpec(
            num_scalar_prefetch=1,
            grid=(pairs,),
            in_specs=[pair_spec] * 5 + [pl.BlockSpec((1, 8, rows), lambda i, *_: (i, 0, 0))],
            out_specs=[pair_spec] * 3,
            scratch_shapes=[pltpu.VMEM((rows, PAIR), F32)],
        ),
        out_shape=[jax.ShapeDtypeStruct((rows, width), BF)] * 3,
        compiler_params=params(),
        name="attend_back",
    )(lengths, q, k, v, out, d_out, lse)


def mlp_kernel(
    att_ref, x_ref, cot_ref, wo_ref, vec_ref, bup_ref, wm_ref,
    hid_ref, dres_ref, datt_ref, go_ref, gm_ref, sums_ref, gbup_ref,
    resid, n_two, mlp, d_norm, act_s, dpre_s,
):
    rows, width = x_ref.shape
    step = pl.program_id(0)
    last = pl.num_programs(0) - 1
    tiles = rows // TILE
    nd, _, block, _ = wm_ref.shape

    def tile(i):
        return pl.ds(pl.multiple_of(i * TILE, TILE), TILE)

    def vec(i):
        return vec_ref[i : i + 1, :]

    @pl.when(step == 0)
    def _():
        def body(i, _):
            r = tile(i)
            res = x_ref[r, :].astype(F32) + dot_nt(att_ref[r, :], wo_ref[0]) + vec(0)
            resid[r, :] = res
            normed, _ = norm_parts(res)
            n_two[r, :] = (normed * vec(1) + vec(2)).astype(BF)
            mlp[r, :] = jnp.zeros((TILE, width), F32)
            d_norm[r, :] = jnp.zeros((TILE, width), F32)
            return 0

        lax.fori_loop(0, tiles, body, 0)

    w_up = wm_ref[:, 0, :, :width].reshape(width, width)
    w_down = wm_ref[:, 0, :, width:].reshape(width, width)
    c_one = 0.7978845608028654
    c_two = 0.044715

    def body(i, total):
        r = tile(i)
        u = dot_nn(n_two[r, :], w_up) + bup_ref[0]
        d_act = dot_nn(cot_ref[r, :], w_down)
        square = u * u
        t = jnp.tanh(c_one * u * (1.0 + c_two * square))
        half = 0.5 * (1.0 + t)
        act = (u * half).astype(BF)
        slope = half + 0.5 * u * (1.0 - t * t) * (c_one * (1.0 + 3.0 * c_two * square))
        d_pre = (d_act * slope).astype(BF)
        act_s[r, :] = act
        dpre_s[r, :] = d_pre
        mlp[r, :] += dot_nt(act, w_down)
        d_norm[r, :] += dot_nt(d_pre, w_up)
        return total + col_sum(d_pre.astype(F32))

    gbup_ref[0] = lax.fori_loop(0, tiles, body, jnp.zeros((1, width), F32))
    per = max(nd // 2, 1)
    for d in range(0, nd, per):
        cols = slice(d * block, (d + per) * block)
        gm_ref[d : d + per, 0, :, :width] = (
            dot_tn(n_two[:, cols], dpre_s[...]).astype(BF).reshape(per, block, width)
        )
        gm_ref[d : d + per, 0, :, width:] = (
            dot_tn(cot_ref[:, cols], act_s[...]).astype(BF).reshape(per, block, width)
        )

    @pl.when(step == last)
    def _():
        def body(i, sums):
            r = tile(i)
            res = resid[r, :]
            hid_ref[r, :] = (res + mlp[r, :] + vec(3)).astype(BF)
            normed, scale = norm_parts(res)
            d_n = d_norm[r, :]
            d_out = cot_ref[r, :].astype(F32)
            d_res = d_out + norm_back(d_n * vec(1), normed, scale)
            dres_ref[r, :] = d_res
            low = d_res.astype(BF)
            act_s[r, :] = low
            datt_ref[r, :] = dot_nn(low, wo_ref[0]).astype(BF)
            more = (col_sum(d_n * normed), col_sum(d_n), col_sum(d_res), col_sum(d_out))
            return tuple(a + b for a, b in zip(sums, more, strict=True))

        sums = lax.fori_loop(0, tiles, body, (jnp.zeros((1, width), F32),) * 4)
        for i in range(4):
            sums_ref[i : i + 1, :] = sums[i]
        half = width // 2
        for c in range(0, width, half):
            go_ref[c : c + half, :] = dot_tn(act_s[:, c : c + half], att_ref[...]).astype(BF)


def feed_forward(att, x, cot, w_all, vecs, b_up, w_mlp):
    rows, width = x.shape
    nd, blocks, block, wide = w_mlp.shape
    whole = once((rows, width), lambda t: (0, 0))
    chunk = pl.BlockSpec((nd, 1, block, wide), lambda t: (0, t, 0, 0))
    up_vec = pl.BlockSpec((1, 1, width), lambda t: (t, 0, 0))
    return pl.pallas_call(
        mlp_kernel,
        grid=(blocks,),
        in_specs=[
            whole,
            whole,
            whole,
            once((1, width, width), lambda t: (3, 0, 0)),
            once((8, width), lambda t: (0, 0)),
            up_vec,
            chunk,
        ],
        out_specs=[
            whole,
            whole,
            whole,
            once((width, width), lambda t: (0, 0)),
            chunk,
            once((8, width), lambda t: (0, 0)),
            up_vec,
        ],
        out_shape=[
            jax.ShapeDtypeStruct((rows, width), BF),
            jax.ShapeDtypeStruct((rows, width), F32),
            jax.ShapeDtypeStruct((rows, width), BF),
            jax.ShapeDtypeStruct((width, width), BF),
            jax.ShapeDtypeStruct(w_mlp.shape, BF),
            jax.ShapeDtypeStruct((8, width), F32),
            jax.ShapeDtypeStruct((blocks, 1, width), F32),
        ],
        scratch_shapes=[
            pltpu.VMEM((rows, width), F32),
            pltpu.VMEM((rows, width), BF),
            pltpu.VMEM((rows, width), F32),
            pltpu.VMEM((rows, width), F32),
            pltpu.VMEM((rows, width), BF),
            pltpu.VMEM((rows, width), BF),
        ],
        compiler_params=params(),
        name="feed_forward",
    )(att, x, cot, w_all, vecs, b_up, w_mlp)


def grad_kernel(blocks, n_ref, dq_ref, dk_ref, dv_ref, go_ref, g_ref):
    per, _, block, _ = g_ref.shape
    rows = per * block
    n_part = n_ref[...]
    full = [dot_tn(n_part, d[...]).astype(BF) for d in (dq_ref, dk_ref, dv_ref)]
    full.append(go_ref[...])

    def put(t, c, value):
        g_ref[:, t, :, c * PAIR : (c + 1) * PAIR] = value.reshape(per, block, PAIR)

    for t in range(blocks):
        for c in range(4):
            put(t, c, full[c][:, t * PAIR : (t + 1) * PAIR])
    for u in range(blocks // 2):
        col = (blocks + u) * PAIR
        for half in range(2):
            left = full[2 * half][:, col : col + PAIR]
            right = full[2 * half + 1][:, col : col + PAIR]
            put(
                2 * u,
                4 + half,
                jnp.concatenate([left[:, :HEAD_DIM], right[:, :HEAD_DIM]], axis=1),
            )
            put(
                2 * u + 1,
                4 + half,
                jnp.concatenate([left[:, HEAD_DIM:], right[:, HEAD_DIM:]], axis=1),
            )


def project_grads(normed, dq, dk, dv, go, shape):
    rows, width = normed.shape
    nd, blocks, block, wide = shape
    parts = 2 if nd > 1 else 1
    part = width // parts
    whole = once((rows, width), lambda i: (0, 0))
    return pl.pallas_call(
        functools.partial(grad_kernel, blocks),
        grid=(parts,),
        in_specs=[
            pl.BlockSpec((rows, part), lambda i: (0, i)),
            whole,
            whole,
            whole,
            pl.BlockSpec((part, width), lambda i: (i, 0)),
        ],
        out_specs=pl.BlockSpec((nd // parts, blocks, block, wide), lambda i: (i, 0, 0, 0)),
        out_shape=jax.ShapeDtypeStruct(shape, BF),
        compiler_params=params(),
        name="project_grads",
    )(normed, dq, dk, dv, go)


def input_kernel(dq_ref, dk_ref, dv_ref, w_ref, x_ref, dres_ref, gain_ref, gin_ref, sums_ref):
    @pl.when(pl.program_id(0) == 0)
    def _():
        sums_ref[...] = jnp.zeros_like(sums_ref)

    d_norm = dot_nt(dq_ref[...], w_ref[0])
    d_norm = d_norm + dot_nt(dk_ref[...], w_ref[1])
    d_norm = d_norm + dot_nt(dv_ref[...], w_ref[2])
    normed, scale = norm_parts(x_ref[...].astype(F32))
    gin_ref[...] = dres_ref[...] + norm_back(d_norm * gain_ref[...], normed, scale)
    more = (
        col_sum(d_norm * normed),
        col_sum(d_norm),
        col_sum(dq_ref[...].astype(F32)),
        col_sum(dv_ref[...].astype(F32)),
    )
    for i, value in enumerate(more):
        sums_ref[i : i + 1, :] += value


def input_grad(dq, dk, dv, w_all, x, d_resid, gain):
    rows, width = x.shape
    row_spec = pl.BlockSpec((TILE, width), lambda i: (i, 0))
    return pl.pallas_call(
        input_kernel,
        grid=(rows // TILE,),
        in_specs=[
            row_spec,
            row_spec,
            row_spec,
            once((3, width, width), lambda i: (0, 0, 0)),
            row_spec,
            row_spec,
            once((1, width), lambda i: (0, 0)),
        ],
        out_specs=[row_spec, pl.BlockSpec((8, width), lambda i: (0, 0))],
        out_shape=[
            jax.ShapeDtypeStruct((rows, width), F32),
            jax.ShapeDtypeStruct((8, width), F32),
        ],
        compiler_params=params(),
        name="input_grad",
    )(dq, dk, dv, w_all, x, d_resid, gain)


def body(
    n_dp,
    n_tensor,
    hidden_in,
    cotangent,
    lengths,
    latent,
    ln1_gain,
    ln1_bias,
    w_qkv,
    b_qv,
    w_out,
    b_out,
    ln2_gain,
    ln2_bias,
    w_up,
    b_up,
    w_down,
    b_down,
):
    rows, width = hidden_in.shape
    t_index = lax.axis_index("tensor")
    block = w_up.shape[0]
    aligned = block % 16 == 0
    heads = w_qkv.shape[2] // HEAD_DIM

    out_t = w_out.T
    packed = jnp.concatenate(
        [w_qkv[0, :, :PAIR], w_qkv[1, :, :PAIR], w_qkv[2, :, :PAIR], out_t[:, :PAIR]]
        + [w_qkv[0, :, PAIR:], w_qkv[1, :, PAIR:], w_qkv[2, :, PAIR:], out_t[:, PAIR:]],
        axis=1,
    ).astype(BF)
    packed_mlp = jnp.concatenate([w_up, w_down.T], axis=1).astype(BF)

    def gather(piece):
        wide = piece.shape[1]
        full = lax.all_gather(piece, BOTH, axis=0, tiled=False)
        full = full.reshape(n_dp, n_tensor, block, wide)
        if aligned:
            return full
        return full.transpose(1, 0, 2, 3).reshape(1, n_tensor, width, wide)

    raw = gather(packed)
    w_mlp = gather(packed_mlp)

    own_length = lax.dynamic_slice_in_dim(lengths, t_index, 1, 0)
    own_latent = lax.dynamic_slice_in_dim(latent, t_index, 1, 0)
    positions = lax.broadcasted_iota(jnp.int32, (1, rows), 1)
    keep = ((positions < own_length) & (own_latent == 0)).astype(BF).reshape(rows, 1)
    cot = cotangent * keep

    def to_inner(b):
        split = b.reshape(b.shape[0], n_tensor, heads, HEAD_DIM)
        return jnp.concatenate(
            [split[:, :, :2].reshape(b.shape[0], -1), split[:, :, 2:].reshape(b.shape[0], -1)],
            axis=1,
        )

    def from_inner(b):
        cut = n_tensor * PAIR
        first = b[:, :cut].reshape(b.shape[0], n_tensor, 2, HEAD_DIM)
        rest = b[:, cut:].reshape(b.shape[0], n_tensor, heads - 2, HEAD_DIM)
        return jnp.concatenate([first, rest], axis=2).reshape(b.shape[0], width)

    q, k, v, normed_one, w_all = project(
        hidden_in, ln1_gain[None], ln1_bias[None], to_inner(b_qv), raw
    )
    attended, lse = attend(own_length, q, k, v)
    zero = jnp.zeros_like(b_out)
    vecs = jnp.stack([b_out, ln2_gain, ln2_bias, b_down, zero, zero, zero, zero])
    hidden_out, d_resid, d_attended, go, gm, sums_two, g_b_up = feed_forward(
        attended, hidden_in, cot, w_all, vecs, b_up.reshape(n_tensor, 1, width), w_mlp
    )
    dq, dk, dv = attend_back(own_length, q, k, v, attended, d_attended, lse)
    ga = project_grads(normed_one, dq, dk, dv, go, raw.shape)
    grad_in, sums_one = input_grad(dq, dk, dv, w_all, hidden_in, d_resid, ln1_gain[None])

    def scatter(grads):
        wide = grads.shape[3]
        if not aligned:
            grads = grads.reshape(n_tensor, n_dp, block, wide).transpose(1, 0, 2, 3)
        flat = grads.reshape(n_dp * n_tensor * block, wide)
        return lax.psum_scatter(flat, BOTH, scatter_dimension=0, tiled=True).astype(F32)

    gm = scatter(gm)
    ga = scatter(ga)
    small = lax.psum(
        jnp.concatenate([sums_one[:4], sums_two[:4], g_b_up.reshape(n_tensor, width)]), BOTH
    )
    g_bqv = from_inner(small[2:4])

    def both_parts(i):
        side = 4 * PAIR + i * HEAD_DIM
        return jnp.concatenate(
            [ga[:, i * PAIR : (i + 1) * PAIR], ga[:, side : side + HEAD_DIM]], axis=1
        )

    return (
        hidden_out,
        grad_in,
        small[0],
        small[1],
        jnp.stack([both_parts(0), both_parts(1), both_parts(2)]),
        g_bqv,
        both_parts(3).T,
        small[6],
        small[4],
        small[5],
        gm[:, :width],
        small[8:].reshape(-1),
        gm[:, width:].T,
        small[7],
    )


def solution(mesh):
    placed = (
        P(BOTH, None),
        P(BOTH, None),
        P("dp"),
        P("dp", None),
        P(),
        P(),
        P(None, "dp", "tensor"),
        P(),
        P("tensor", "dp"),
        P(),
        P(),
        P(),
        P("dp", "tensor"),
        P(),
        P("tensor", "dp"),
        P(),
    )
    return jax.shard_map(
        functools.partial(body, mesh.shape["dp"], mesh.shape["tensor"]),
        mesh=mesh,
        in_specs=placed,
        out_specs=(
            P(BOTH, None),
            P(BOTH, None),
            P(),
            P(),
            P(None, "dp", "tensor"),
            P(),
            P("tensor", "dp"),
            P(),
            P(),
            P(),
            P("dp", "tensor"),
            P(),
            P("tensor", "dp"),
            P(),
        ),
        check_vma=False,
    )
```

time: 876 us -> 514 us (0.59)
  matrix products: 235 us -> 0 us
  Pallas kernels: 0 us -> 138 us
  other arithmetic: 97.7 us -> 7.02 us
  blocking collectives: 116 us -> 39.7 us
  local copies, waits for them, and re-layouts: 67.7 us -> 10.9 us
  waiting for transfers between devices: 337 us -> 303 us
    dot_general x24 -> x0, matrix products: 235 us -> none  [the longest x2 36.9 us: attend_backward(): jnp.einsum('qhd,khd->hqk', dout_block, v_heads, preferred_element_type=jn...]
    pallas_call x0 -> x6, Pallas kernels: none -> 138 us  [the longest x1 53.1 us: feed_forward(): pl.pallas_call(mlp_kernel, grid=(blocks,), in_specs=[whole, whole, whole,...]
    all_gather x2 -> x0, blocking collectives: 74.9 us -> none  [the longest x1 43.5 us: body(): lax.all_gather(w_qkv.astype(jnp.bfloat16), 'dp', axis=1, tiled=True)]
    all_gather x6 -> x2, waiting for transfers between devices: 38.4 us -> 111 us  [gather(): full = lax.all_gather(piece, BOTH, axis=0, tiled=False)]
    unnamed x17 -> x5, waiting for transfers between devices: 123 us -> 52.9 us
    convert_element_type x7 -> x1, other arithmetic: 50.3 us -> 1.08 us  [scatter(): lax.psum_scatter(flat, BOTH, scatter_dimension=0, tiled=True).astype(F32)]
    unnamed x124 -> x32, local copies, waits for them, and re-layouts: 45.1 us -> 3.06 us
    reduce_sum x12 -> x0, other arithmetic: 38.8 us -> none  [the longest x2 26.6 us: attend_forward(): totals = jnp.sum(shifted, axis=-1, keepdims=True)]
  transfers between devices with their start and end apart: 14 -> 4, of which waited for: 8 -> 4; matrix products, arithmetic and copies ran while one was open for 35% -> 2% of each run, Pallas kernels for 0% -> 9%
where the time goes in v1:
time: 514 us
  waiting for transfers between devices  303 us (59%)
  Pallas kernels  138 us (27%)
  blocking collectives  39.7 us (8%)
  between operations  14.1 us (3%)
  local copies, waits for them, and re-layouts  10.9 us (2%)
  other arithmetic  7.02 us (1%)
    reduce_scatter x1, waiting for transfers between devices, scatter(): lax.psum_scatter(flat, BOTH, scatter_dimension=0, tiled=True).astype(F32)  139 us
    all_gather x2, waiting for transfers between devices, gather(): full = lax.all_gather(piece, BOTH, axis=0, tiled=False)  111 us
    pallas_call x1, Pallas kernels, feed_forward(): pl.pallas_call(mlp_kernel, grid=(blocks,), in_specs=[whole, whole, whole,...  53.1 us
    unnamed x5, waiting for transfers between devices  52.9 us
    psum x1, blocking collectives, body(): lax.psum(jnp.concatenate([sums_one[:4], sums_two[:4], g_b_up.reshape(n_te...  39.7 us
    pallas_call x1, Pallas kernels, attend_back(): pl.pallas_call(attend_back_kernel, grid_spec=pltpu.PrefetchScalarGridSpec...  33 us
    pallas_call x1, Pallas kernels, attend(): pl.pallas_call(attend_kernel, grid_spec=pltpu.PrefetchScalarGridSpec(num_...  22.2 us
    pallas_call x1, Pallas kernels, project(): pl.pallas_call(functools.partial(qkv_kernel, blocks), grid=(rows // TILE,...  11.3 us
  transfers between devices with their start and end apart: 4, of which 4 were waited for; matrix products, arithmetic and copies ran while one was open for 2% of the time, Pallas kernels for 9%

profile of v1, /device:TPU:0, one launch (start us, length us, event | category | flops | bytes accessed | tf_op | source)
XLA Modules:
  0.0 513.5 jit_solution(16884607579615950304)
XLA Ops:
  7.2 1.0 copy.41
  8.4 1.1 convert.32
  9.6 0.8 concatenate.54
  10.5 0.7 pad_maximum_fusion
  14.1 1.4 fusion
  16.1 1.3 broadcast_multiply_fusion.cot_ref
  17.4 60.4 %all-gather.3.cloned.1.call-done = bf16[32,96,768]{2,1,0:T(8,128)(2,1)} async-done(((bf16[1,96,768]{2,1,0:T(8,128)(2,1)}), bf16[32,96,768]{2,1,0:T(8,128)(2,1)}) %all-gather.3.cloned.1.call-update) | async-done | bytes 4718608 | tf_op jit(solution)/shard_map/all_gather | solution.py:516
  77.8 11.3 %project.1 = (bf16[1024,768]{1,0:T(8,128)(2,1)}, bf16[1024,768]{1,0:T(8,128)(2,1)}, bf16[1024,768]{1,0:T(8,128)(2,1)}, bf16[1024,768]{1,0:T(8,128)(2,1)}, bf16[4,768,768]{2,1,0:T(8,128)(2,1)}) custom-call(bf16[1024,768]{1,0:T(8,128)(2,1)} %x_ref.5, f32[1,768]{1,0:T(1,128)} %broadcast_in_dim.8.gain_ref, f32[1,768]{1,0:T(1,128)} %broadcast_in_dim.9.bias_ref, ...), custom_call_target="tpu_custom_call" | custom-call | tf_op jit(solution)/shard_map/project/pallas_call | solution.py:97
  89.1 22.2 %attend.1 = (bf16[1024,768]{1,0:T(8,128)(2,1)}, f32[6,8,1024]{2,1,0:T(8,128)}) custom-call(s32[1]{0:T(128)} %dynamic_slice.6.len_ref, bf16[1024,768]{1,0:T(8,128)(2,1)} %get-tuple-element.33.q_ref, bf16[1024,768]{1,0:T(8,128)(2,1)} %get-tuple-element.34.k_ref, bf16[1024,768]{1,0:T(8,128)(2,1)} %get-tuple-element.35.v_ref), custom_call_target="tpu_custom_call" | custom-call | tf_op jit(solution)/shard_map/attend/pallas_call | solution.py:161
  111.3 51.1 %all-gather.5.cloned.1.call-done = bf16[32,96,1536]{2,1,0:T(8,128)(2,1)} async-done(((bf16[1,96,1536]{2,1,0:T(8,128)(2,1)}), bf16[32,96,1536]{2,1,0:T(8,128)(2,1)}) %all-gather.5.cloned.1.call-update) | async-done | bytes 9437200 | tf_op jit(solution)/shard_map/all_gather | solution.py:516
  162.3 53.1 %feed_forward.1 = (bf16[1024,768]{1,0:T(8,128)(2,1)}, f32[1024,768]{1,0:T(8,128)}, bf16[1024,768]{1,0:T(8,128)(2,1)}, bf16[768,768]{1,0:T(8,128)(2,1)}, bf16[8,4...) custom-call(bf16[1024,768]{1,0:T(8,128)(2,1)} %get-tuple-element.36.att_ref.o_ref, ...), custom_call_target="tpu_custom_call" | custom-call | tf_op jit(solution)/shard_map/feed_forward/pallas_call | solution.py:339
  215.5 33.0 %attend_back.1 = (bf16[1024,768]{1,0:T(8,128)(2,1)}, bf16[1024,768]{1,0:T(8,128)(2,1)}, bf16[1024,768]{1,0:T(8,128)(2,1)}) custom-call(s32[1]{0:T(128)} %dynamic_slice.6.len_ref, bf16[1024,768]{1,0:T(8,128)(2,1)} %get-tuple-element.33.q_ref, bf16[1024,768]{1,0:T(8,128)(2,1)} %get-tuple-element.34.k_ref, bf16[1024,768]{1,0:T(8,128)(2,1)} %get-tuple-element.35.v_ref, ...), custom_call_target="tpu_custom_call" | custom-call | tf_op jit(solution)/shard_map/attend_back/pallas_call | solution.py:230
  248.4 8.6 %project_grads.1 = bf16[8,4,96,768]{3,2,1,0:T(8,128)(2,1)} custom-call(bf16[1024,768]{1,0:T(8,128)(2,1)} %get-tuple-element.49.n_ref, bf16[1024,768]{1,0:T(8,128)(2,1)} %get-tuple-element.41.dq_ref, bf16[1024,768]{1,0:T(8,128)(2,1)} %get-tuple-element.42.dk_ref, bf16[1024,768]{1,0:T(8,128)(2,1)} %get-tuple-element.43.dv_ref, ...), custom_call_target="tpu_custom_call" | custom-call | tf_op jit(solution)/shard_map/project_grads/pallas_call | solution.py:418
  257.6 10.3 %input_grad.1 = (f32[1024,768]{1,0:T(8,128)}, f32[8,768]{1,0:T(8,128)}) custom-call(bf16[1024,768]{1,0:T(8,128)(2,1)} %get-tuple-element.41.dq_ref, bf16[1024,768]{1,0:T(8,128)(2,1)} %get-tuple-element.42.dk_ref, bf16[1024,768]{1,0:T(8,128)(2,1)} %get-tuple-element.43.dv_ref, bf16[4,768,768]{2,1,0:T(8,128)(2,1)} %get-tuple-element.37.wo_ref.w_ref, ...), custom_call_target="tpu_custom_call" | custom-call | tf_op jit(solution)/shard_map/input_grad/pallas_call | solution.py:458
  267.9 0.7 slice.114
  268.7 39.7 %psum.7 = f32[12,768]{1,0:T(8,128)S(1)} all-reduce(f32[12,768]{1,0:T(8,128)S(1)} %pad_maximum_fusion.2), channel_id=1, replica_groups=mesh['dp'=8,'tensor'=4] {'dp','tensor'}, use_global_device_ids=true, to_apply=%region_0.0 | all-reduce | flops 9216 | bytes 73728 | tf_op jit(solution)/shard_map/psum | solution.py:566
  308.7 0.7 reshape.218
  310.6 52.3 %reduce-scatter.7.cloned.1.call-done = bf16[96,768]{1,0:T(8,128)(2,1)} async-done(((bf16[3072,768]{1,0:T(8,128)(2,1)}), bf16[96,768]{1,0:T(8,128)(2,1)}) %reduce-scatter.7.cloned.1.call-update) | async-done | bytes 147472
  362.9 1.1 copy.46
  364.1 0.9 copy.44
  365.7 138.8 %reduce-scatter.5.cloned.1.call-done = bf16[96,1536]{1,0:T(8,128)(2,1)} async-done(((bf16[3072,1536]{1,0:T(8,128)(2,1)}), bf16[96,1536]{1,0:T(8,128)(2,1)}) %reduce-scatter.5.cloned.1.call-update) | async-done | bytes 294928 | tf_op jit(solution)/shard_map/reduce_scatter | solution.py:562
  504.4 1.1 convert_element_type.24
  505.5 0.7 slice_bitcast_fusion
  506.3 0.7 slice.160
  (74 shorter events, 6.4 us)
Async XLA Ops:
  7.2 3.2 copy-start.2
  7.2 3.3 copy-start.3
  7.2 70.6 %all-gather.3.cloned.1.call-start = ((), (), s32[]{:S(2)}) async-start(), calls=%async_computation.2 | async-start | bytes 4866048 | tf_op jit(solution)/shard_map/all_gather | solution.py:516
  8.3 3.0 copy-start.7
  8.3 3.6 copy-start.8
  8.3 4.2 copy-start.9
  8.3 4.2 copy-start.10
  8.3 4.2 copy-start.11
  8.3 4.2 copy-start.12
  8.4 4.2 copy-start.6
  8.4 4.4 copy-start.13
  8.4 7.7 %copy-start = (bf16[1024,768]{1,0:T(8,128)(2,1)S(1)}, bf16[1024,768]{1,0:T(8,128)(2,1)}, u32[]{:S(2)}) copy-start(bf16[1024,768]{1,0:T(8,128)(2,1)} %param.17) | copy-start | bytes 4718596
  10.4 152.0 %all-gather.5.cloned.1.call-start = ((), (), s32[]{:S(2)}) async-start(), calls=%async_computation.3 | async-start | bytes 9732096 | tf_op jit(solution)/shard_map/all_gather | solution.py:516
  11.2 351.7 %reduce-scatter.7.cloned.1.call-start = ((), (), s32[]{:S(2)}) async-start(), calls=%async_computation.5 | async-start | bytes 4866048
  257.0 247.4 %reduce-scatter.5.cloned.1.call-start = ((), (), s32[]{:S(2)}) async-start(), calls=%async_computation.4 | async-start | bytes 9732096 | tf_op jit(solution)/shard_map/reduce_scatter | solution.py:562
  257.6 11.1 %copy-start.5 = (f32[8,768]{1,0:T(8,128)S(1)}, f32[8,768]{1,0:T(8,128)}, u32[]{:S(2)}) copy-start(f32[8,768]{1,0:T(8,128)} %get-tuple-element.47) | copy-start | bytes 73732
  257.6 11.1 %copy-start.4 = (f32[4,1,768]{2,1,0:T(1,128)S(1)}, f32[4,1,768]{2,1,0:T(1,128)}, u32[]{:S(2)}) copy-start(f32[4,1,768]{2,1,0:T(1,128)} %get-tuple-element.48) | copy-start | bytes 36868
  504.4 1.8 copy-start.1
Sparse Core Ops, SparseCore 0:
  11.5 66.2 all-gather.2
  81.3 80.9 all-gather.4
  257.1 105.7 reduce-scatter.6
  369.7 134.6 reduce-scatter.4
